TPU v7x, 256 devices: a whole 4x4x8 slice. The times are simulated.
256 devices in a mesh: gx: 8 (over z), gy: 4 (over y_lo, core), gz: 8 (over y_hi, x).
Axes of the slice: x: 4, y: 4 (y_hi: 2, y_lo: 2; y = y_hi * 2 + y_lo), z: 8, core: 2. Of those that a mesh axis runs over, the one named last changes fastest.
Arguments:
- state: bfloat16 [128, 64, 16, 8, 128], P('gx', 'gy', 'gz'), may hold values from -6 to 6
- cotangent: bfloat16 [128, 64, 16, 8, 128], P('gx', 'gy', 'gz'), may hold values from -6 to 6
- counts: int32 [8], P('gz'), may hold values from 1 to 2, 12 in all
- edge_weights: bfloat16 [2, 2, 128, 128], replicated, may hold values from -0.5 to 0.5
- node_in: bfloat16 [2, 256, 128], replicated, may hold values from -0.375 to 0.375
- node_out: bfloat16 [2, 128, 128], replicated, may hold values from -0.5 to 0.5
- biases: float32 [2, 2, 128], replicated, may hold values from -4 to 4
Outputs:
- state_grad: bfloat16 [128, 64, 16, 8, 128], P('gx', 'gy', 'gz')
- edge_grads: float32 [2, 2, 128, 128], replicated
- node_in_grad: float32 [2, 256, 128], replicated
- node_out_grad: float32 [2, 128, 128], replicated
- bias_grads: float32 [2, 2, 128], replicated
Inputs may be any that keep to these rules, and one draw needn't show every extreme that they name: The counts sum to 12; index k of gz holds the element layers that follow those of smaller indices.
All inputs are finite; a program needn't handle non-finite values. No bound on the sum of `counts` on one device may be relied on, other than what follows from the above.
Results may differ from a plain program's by a relative error of at most 0.012.
The roundings to bfloat16 on the way count: a program that leaves them out, or rounds other values in their place, can miss the bound.
Values sent between devices are 32-bit elements; how exact they have to be, the bound alone decides.
A program may use at most 128 MiB of HBM per device.

v0:
```python
import math
import jax
import jax.numpy as jnp
from jax import lax
from jax.sharding import PartitionSpec as P

edge_dims = (1, 3, 5)


def with_halo(cells, sides, width):
    for axis, dim in sides:
        count = lax.axis_size(axis)
        ends = count - 1
        head = lax.slice_in_dim(cells, 0, width, axis=dim)
        tail = lax.slice_in_dim(cells, cells.shape[dim] - width, cells.shape[dim], axis=dim)
        cells = jnp.concatenate(
            [
                lax.ppermute(tail, axis, [(i, (i + 1) % count) for i in range(ends)]),
                cells,
                lax.ppermute(head, axis, [((i + 1) % count, i) for i in range(ends)]),
            ],
            axis=dim,
        )
    return cells


def slice_along(array, start, stop, dim_no):
    return lax.slice_in_dim(array, start, stop, axis=dim_no)


def matmul_rows(left, weight):
    flattened = left.reshape(-1, left.shape[-1])
    product = jnp.dot(flattened, weight, preferred_element_type=jnp.float32)
    return product.reshape(left.shape[:-1] + (weight.shape[-1],))


def cross_rows(left, right):
    return lax.dot_general(
        left.reshape(-1, left.shape[-1]),
        right.reshape(-1, right.shape[-1]),
        (((0,), (0,)), ((), ())),
        preferred_element_type=jnp.float32,
    )


def spread_diff(values, dim_no):
    zero_row = jnp.zeros_like(slice_along(values, 0, 1, dim_no))
    return jnp.concatenate([zero_row, values], dim_no) - jnp.concatenate([values, zero_row], dim_no)


def silu_slope(values):
    sig_value = jax.nn.sigmoid(values)
    return sig_value * (1.0 + values * (1.0 - sig_value))


def edges_forward(features, weight_one, weight_two, bias_edge):
    widened = features.astype(jnp.float32)
    messages = jnp.zeros(features.shape, jnp.float32)
    stored = []
    for dim_no in edge_dims:
        length = features.shape[dim_no]
        differ = (
            slice_along(widened, 1, length, dim_no) - slice_along(widened, 0, length - 1, dim_no)
        ).astype(jnp.bfloat16)
        before = matmul_rows(differ, weight_one) + bias_edge
        active = jax.nn.silu(before).astype(jnp.bfloat16)
        messages = messages + spread_diff(matmul_rows(active, weight_two), dim_no)
        stored.append((differ, before, active))
    return (messages, stored)


def edges_backward(grad_msg, stored, weight_one, weight_two):
    feat_width = grad_msg.shape[-1]
    grad_feat = jnp.zeros(grad_msg.shape, jnp.float32)
    grad_one = jnp.zeros((feat_width, feat_width), jnp.float32)
    grad_two = jnp.zeros((feat_width, feat_width), jnp.float32)
    grad_bias = jnp.zeros((feat_width,), jnp.float32)
    for dim_no, entry in zip(edge_dims, stored):
        differ, before, active = entry
        length = grad_msg.shape[dim_no]
        grad_out = (
            slice_along(grad_msg, 1, length, dim_no) - slice_along(grad_msg, 0, length - 1, dim_no)
        ).astype(jnp.bfloat16)
        grad_two = grad_two + cross_rows(active, grad_out)
        grad_pre = (matmul_rows(grad_out, weight_two.T) * silu_slope(before)).astype(jnp.bfloat16)
        grad_one = grad_one + cross_rows(differ, grad_pre)
        grad_bias = grad_bias + jnp.sum(grad_pre.astype(jnp.float32).reshape(-1, feat_width), 0)
        grad_feat = grad_feat + spread_diff(matmul_rows(grad_pre, weight_one.T), dim_no)
    return (grad_feat, grad_one, grad_two, grad_bias)


def node_forward(features, summed, weight_in, weight_out, bias_node):
    joined = jnp.concatenate([features, summed.astype(jnp.bfloat16)], -1)
    before = matmul_rows(joined, weight_in) + bias_node
    active = jax.nn.silu(before).astype(jnp.bfloat16)
    result = (features.astype(jnp.float32) + matmul_rows(active, weight_out)).astype(jnp.bfloat16)
    return (result, (joined, before, active))


def node_backward(grad_next, stored, weight_in, weight_out):
    joined, before, active = stored
    feat_width = grad_next.shape[-1]
    grad_out_w = cross_rows(active, grad_next)
    grad_pre = (matmul_rows(grad_next, weight_out.T) * silu_slope(before)).astype(jnp.bfloat16)
    grad_in_w = cross_rows(joined, grad_pre)
    grad_bias = jnp.sum(grad_pre.astype(jnp.float32).reshape(-1, feat_width), 0)
    grad_joined = matmul_rows(grad_pre, weight_in.T)
    grad_feat = grad_next.astype(jnp.float32) + grad_joined[..., :feat_width]
    return (grad_feat, grad_joined[..., feat_width:], grad_in_w, grad_out_w, grad_bias)


def couple(array, elem_dim, node_dim):
    moved = jnp.moveaxis(array, (elem_dim, node_dim), (0, 1))
    front_face = moved[:, 0]
    back_face = moved[:, -1]
    zero_face = jnp.zeros_like(front_face[:1])
    new_front = front_face + jnp.concatenate([zero_face, back_face[:-1]], 0)
    new_back = back_face + jnp.concatenate([front_face[1:], zero_face], 0)
    joined = jnp.concatenate([new_front[:, None], moved[:, 1:-1], new_back[:, None]], 1)
    return jnp.moveaxis(joined, (0, 1), (elem_dim, node_dim))


def local_couple(values, dim_no, nodes_edge):
    full_shape = values.shape
    elems_here = full_shape[dim_no] // nodes_edge
    split_shape = full_shape[:dim_no] + (elems_here, nodes_edge) + full_shape[dim_no + 1 :]
    return couple(values.reshape(split_shape), dim_no, dim_no + 1).reshape(full_shape)


def fold_rim(extended, dim_no):
    inner_len = extended.shape[dim_no] - 2
    core_rows = slice_along(extended, 1, inner_len + 1, dim_no)
    front_row = slice_along(core_rows, 0, 1, dim_no) + slice_along(extended, 0, 1, dim_no)
    back_row = slice_along(core_rows, inner_len - 1, inner_len, dim_no) + slice_along(
        extended, inner_len + 1, inner_len + 2, dim_no
    )
    return jnp.concatenate(
        [front_row, slice_along(core_rows, 1, inner_len - 1, dim_no), back_row], dim_no
    )


def on_device(state, cotangent, counts, edge_weights, node_in, node_out, biases):
    nodes_edge = state.shape[3]
    span_x = state.shape[0]
    span_y = state.shape[1]
    elems_x = span_x // nodes_edge
    elems_y = span_y // nodes_edge
    slot_count = state.shape[2]
    grid_shape = state.shape[:4]
    filled = counts[0]
    slot_ids = jnp.arange(slot_count, dtype=jnp.int32)
    node_ids = jnp.arange(nodes_edge, dtype=jnp.int32)
    live_mask = (slot_ids < filled).astype(jnp.float32)[None, None, :, None, None]

    def edge_mult(position, axis_len, elems_here):
        place = jnp.arange(elems_here * nodes_edge, dtype=jnp.int32)
        node_here = place % nodes_edge
        elem_global = position * elems_here + place // nodes_edge
        front_pair = ((node_here == 0) & (elem_global > 0)).astype(jnp.float32)
        back_pair = (
            (node_here == nodes_edge - 1) & (elem_global < elems_here * axis_len - 1)
        ).astype(jnp.float32)
        return 1.0 + front_pair + back_pair

    mult_x = edge_mult(lax.axis_index("gx"), lax.axis_size("gx"), elems_x)
    mult_y = edge_mult(lax.axis_index("gy"), lax.axis_size("gy"), elems_y)
    index_z = lax.axis_index("gz")
    size_z = lax.axis_size("gz")
    lower_mult = ((slot_ids > 0) | (index_z > 0)).astype(jnp.float32)
    upper_mult = ((slot_ids < filled - 1) | (index_z < size_z - 1)).astype(jnp.float32)
    mult_z = (
        1.0
        + (node_ids == 0).astype(jnp.float32)[None, :] * lower_mult[:, None]
        + (node_ids == nodes_edge - 1).astype(jnp.float32)[None, :] * upper_mult[:, None]
    )
    copies = (
        mult_x[:, None, None, None, None]
        * mult_y[None, :, None, None, None]
        * mult_z[None, None, :, :, None]
    )

    def couple_all(values):
        inner = local_couple(local_couple(values, 0, nodes_edge), 1, nodes_edge)
        extended = with_halo(inner, (("gx", 0), ("gy", 1)), 1)
        coupled = fold_rim(fold_rim(extended, 0), 1)
        top_faces = coupled[:, :, :, -1]
        bottom_faces = coupled[:, :, :, 0]
        top_used = lax.dynamic_index_in_dim(top_faces, filled - 1, 2, keepdims=False)
        rim_pair = jnp.stack([bottom_faces[:, :, 0], top_used], 2)
        rim_ext = with_halo(rim_pair, (("gz", 2),), 1)
        from_below = rim_ext[:, :, 0]
        from_above = rim_ext[:, :, 3]
        below_add = jnp.concatenate([from_below[:, :, None], top_faces[:, :, :-1]], 2)
        last_slot = (slot_ids == filled - 1).astype(jnp.float32)[None, None, :, None]
        above_add = (
            jnp.concatenate([bottom_faces[:, :, 1:], jnp.zeros_like(bottom_faces[:, :, :1])], 2)
            + last_slot * from_above[:, :, None]
        )
        result = jnp.concatenate(
            [
                (bottom_faces + below_add)[:, :, :, None],
                coupled[:, :, :, 1:-1],
                (top_faces + above_add)[:, :, :, None],
            ],
            3,
        )
        return result * live_mask

    def to_cells(array):
        return array.reshape(
            (elems_x, nodes_edge, elems_y, nodes_edge, slot_count, nodes_edge, array.shape[-1])
        )

    def to_grid(array):
        return array.reshape(grid_shape + (array.shape[-1],))

    features = state
    grad_next = cotangent * live_mask.astype(jnp.bfloat16)
    saved = []
    for layer_no in range(2):
        messages, edge_store = edges_forward(
            to_cells(features),
            edge_weights[layer_no, 0],
            edge_weights[layer_no, 1],
            biases[layer_no, 0],
        )
        summed = couple_all(to_grid(messages) * live_mask) / copies
        result, node_store = node_forward(
            features, summed, node_in[layer_no], node_out[layer_no], biases[layer_no, 1]
        )
        saved.append((edge_store, node_store))
        features = result
    per_layer = [None, None]
    for layer_no in (1, 0):
        edge_store, node_store = saved[layer_no]
        grad_feat, grad_sum, grad_in_w, grad_out_w, grad_node_b = node_backward(
            grad_next, node_store, node_in[layer_no], node_out[layer_no]
        )
        grad_msg = couple_all(grad_sum / copies * live_mask)
        grad_edge, grad_one, grad_two, grad_edge_b = edges_backward(
            to_cells(grad_msg), edge_store, edge_weights[layer_no, 0], edge_weights[layer_no, 1]
        )
        grad_next = (grad_feat + to_grid(grad_edge)).astype(jnp.bfloat16)
        local_terms = (
            jnp.stack([grad_one, grad_two]),
            grad_in_w,
            grad_out_w,
            jnp.stack([grad_edge_b, grad_node_b]),
        )
        per_layer[layer_no] = local_terms
    stacked = tuple(
        (jnp.stack([per_layer[0][pos_no], per_layer[1][pos_no]]) for pos_no in range(4))
    )
    stacked = lax.psum(stacked, ("gx", "gy", "gz"))
    layers_all = 3 * slot_count * size_z // 4
    nodes_all = (
        nodes_edge**3 * elems_x * lax.axis_size("gx") * elems_y * lax.axis_size("gy") * layers_all
    )
    grad_scale = 1.0 / math.sqrt(nodes_all)
    state_grad = grad_next * live_mask.astype(jnp.bfloat16)
    return (
        state_grad,
        stacked[0] * grad_scale,
        stacked[1] * grad_scale,
        stacked[2] * grad_scale,
        stacked[3] * grad_scale,
    )


def solution(mesh):
    return jax.shard_map(
        on_device,
        mesh=mesh,
        in_specs=(
            P("gx", "gy", "gz", None, None),
            P("gx", "gy", "gz", None, None),
            P("gz"),
            P(),
            P(),
            P(),
            P(),
        ),
        out_specs=(P("gx", "gy", "gz", None, None), P(), P(), P(), P()),
        check_vma=False,
    )
```

profile of v0, /device:TPU:1, one launch (start us, length us, event | category | flops | bytes accessed | tf_op | source)
XLA Modules:
  0.0 601.1 jit_solution(5968325419626531154)
XLA Ops:
  27.5 4.4 collective-permute-start
  40.3 4.7 collective-permute-start.2
  47.4 4.4 collective-permute-done.3
  63.2 4.5 collective-permute-done.5
  88.6 3.6 collective-permute-start.6
  94.8 5.2 collective-permute-done.7
  100.2 4.2 collective-permute-start.8
  106.5 4.4 collective-permute-done.9
  112.7 3.6 collective-permute-start.10
  121.6 3.5 collective-permute-done.11
  133.8 4.6 collective-permute-start.12
  140.9 4.1 collective-permute-done.13
  145.3 4.2 collective-permute-start.14
  152.4 3.6 collective-permute-done.15
  157.7 5.7 collective-permute-start.16
  168.5 3.4 collective-permute-done.17
  192.4 3.6 collective-permute-start.18
  199.0 3.5 collective-permute-done.19
  202.7 4.2 collective-permute-start.20
  209.5 3.8 collective-permute-done.21
  215.2 7.3 %collective-permute-start.22 = (f32[16,16,1,128]{3,1,0,2:T(8,128)S(1)}, f32[16,16,1,128]{3,1,0,2:T(8,128)S(1)}, u32[]{:S(2)}, u32[]{:S(2)}) collective-permute-start(f32[16,16,1,128]{3,1,0,2:T(8,128)S(1)} %dynamic-slice_bitcast_fusion), channel_id=1, source_target_pairs={{0,1},{1,2},{2,3},{3,4},{4,5},{5,6},{6,7},{8,9},{9,10},{10,11},{11... | collective-permute-start | bytes 393224 | tf_op jit(solution)/shard_map/ppermute | solution.py:18
  246.3 84.3 %psum.31 = f32[2,2,128]{2,1,0:T(2,128)S(1)} all-reduce(f32[2,2,128]{2,1,0:T(2,128)S(1)} %pad_maximum_fusion.51), channel_id=1, replica_groups=mesh['gx'=8,'gy'=4,'gz'=8] {'gx','gy','gz'}, use_global_device_ids=true, to_apply=%region_11.12 | all-reduce | flops 512 | bytes 4096 | tf_op jit(solution)/shard_map/psum | solution.py:254
  336.7 4.3 subtract_add_fusion
  342.6 246.3 %all-reduce.47.cloned.1.call-done = (f32[2,2,128,128]{3,2,1,0:T(8,128)}, f32[2,256,128]{2,1,0:T(8,128)}, f32[2,128,128]{2,1,0:T(8,128)}) async-done(((f32[2,2,128,128]{3,2,1,0:T(8,128)}, f32[2,256,128]{2,1,0:T(8,128)}, f32[2,128,128]{2,1,0:T(8,128)}), (f32[2,2,128,128]{3,2,1,0:T(8,128)}, f32[2,256,128]{2,1,0:T(8,128)}, f32[2,128,128]{2,1,0:T(8,128)})) %all-reduce.47.cloned.1.call-update) | async-done | bytes 655376 | tf_op jit(solution)/shard_map/psum | solution.py:254
  (340 shorter events, 158.7 us)
Async XLA Ops:
  7.2 581.7 %all-reduce.47.cloned.1.call-start = ((), (), s32[]{:S(2)}) async-start(), calls=%async_computation | async-start | bytes 1310720 | tf_op jit(solution)/shard_map/psum | solution.py:254
  27.5 8.1 %collective-permute-start = (f32[1,16,2,8,128]{4,1,0,3,2:T(8,128)}, f32[1,16,2,8,128]{4,1,0,3,2:T(8,128)S(1)}, u32[]{:S(2)}, u32[]{:S(2)}) collective-permute-start(f32[1,16,2,8,128]{4,1,0,3,2:T(8,128)} %get-tuple-element.56), channel_id=1, source_target_pairs={{0,32},{32,64},{64,96},{96,128},{128,160},{160,192},{192,224},{1,3... | collective-permute-start | bytes 393224 | tf_op jit(solution)/shard_map/ppermute | solution.py:18
  31.8 6.7 %collective-permute-start.1 = (f32[1,16,2,8,128]{4,1,0,3,2:T(8,128)}, f32[1,16,2,8,128]{4,1,0,3,2:T(8,128)}, u32[]{:S(2)}, u32[]{:S(2)}) collective-permute-start(f32[1,16,2,8,128]{4,1,0,3,2:T(8,128)} %get-tuple-element.57), channel_id=1, source_target_pairs={{32,0},{64,32},{96,64},{128,96},{160,128},{192,160},{224,192},{33,... | collective-permute-start | bytes 393224 | tf_op jit(solution)/shard_map/ppermute | solution.py:20
  40.3 7.1 %collective-permute-start.2 = (f32[18,1,2,8,128]{4,1,0,3,2:T(1,128)}, f32[18,1,2,8,128]{4,1,0,3,2:T(1,128)S(1)}, u32[]{:S(2)}, u32[]{:S(2)}) collective-permute-start(f32[18,1,2,8,128]{4,1,0,3,2:T(1,128)} %get-tuple-element.30), channel_id=1, source_target_pairs={{0,8},{8,16},{16,24},{1,9},{9,17},{17,25},{2,10},{10,18},{18,26},{... | collective-permute-start | bytes 442376 | tf_op jit(solution)/shard_map/ppermute | solution.py:18
  45.0 6.8 %collective-permute-start.3 = (f32[18,1,2,8,128]{4,1,0,3,2:T(1,128)}, f32[18,1,2,8,128]{4,1,0,3,2:T(1,128)}, u32[]{:S(2)}, u32[]{:S(2)}) collective-permute-start(f32[18,1,2,8,128]{4,1,0,3,2:T(1,128)} %get-tuple-element.31), channel_id=1, source_target_pairs={{8,0},{16,8},{24,16},{9,1},{17,9},{25,17},{10,2},{18,10},{26,18},{... | collective-permute-start | bytes 442376 | tf_op jit(solution)/shard_map/ppermute | solution.py:20
  61.6 6.1 %collective-permute-start.5 = (f32[16,16,1,128]{3,1,0,2:T(8,128)S(1)}, f32[16,16,1,128]{3,1,0,2:T(8,128)S(1)}, u32[]{:S(2)}, u32[]{:S(2)}) collective-permute-start(f32[16,16,1,128]{3,1,0,2:T(8,128)S(1)} %get-tuple-element.76), channel_id=1, source_target_pairs={{1,0},{2,1},{3,2},{4,3},{5,4},{6,5},{7,6},{9,8},{10,9},{11,10},{12... | collective-permute-start | bytes 393224 | tf_op jit(solution)/shard_map/ppermute | solution.py:20
  88.6 6.2 %collective-permute-start.6 = (f32[1,16,2,8,128]{4,1,0,2,3:T(8,128)S(1)}, f32[1,16,2,8,128]{4,1,0,2,3:T(8,128)S(1)}, u32[]{:S(2)}, u32[]{:S(2)}) collective-permute-start(f32[1,16,2,8,128]{4,1,0,2,3:T(8,128)S(1)} %get-tuple-element.48), channel_id=1, source_target_pairs={{0,32},{32,64},{64,96},{96,128},{128,160},{160,192},{192,224},{1,3... | collective-permute-start | bytes 393224 | tf_op jit(solution)/shard_map/ppermute | solution.py:18
  92.2 7.8 %collective-permute-start.7 = (f32[1,16,2,8,128]{4,1,0,2,3:T(8,128)S(1)}, f32[1,16,2,8,128]{4,1,0,2,3:T(8,128)S(1)}, u32[]{:S(2)}, u32[]{:S(2)}) collective-permute-start(f32[1,16,2,8,128]{4,1,0,2,3:T(8,128)S(1)} %get-tuple-element.49), channel_id=1, source_target_pairs={{32,0},{64,32},{96,64},{128,96},{160,128},{192,160},{224,192},{33,... | collective-permute-start | bytes 393224 | tf_op jit(solution)/shard_map/ppermute | solution.py:20
  100.2 6.3 %collective-permute-start.8 = (f32[18,1,2,8,128]{4,1,0,2,3:T(1,128)S(1)}, f32[18,1,2,8,128]{4,1,0,2,3:T(1,128)S(1)}, u32[]{:S(2)}, u32[]{:S(2)}) collective-permute-start(f32[18,1,2,8,128]{4,1,0,2,3:T(1,128)S(1)} %get-tuple-element.28), channel_id=1, source_target_pairs={{0,8},{8,16},{16,24},{1,9},{9,17},{17,25},{2,10},{10,18},{18,26},{... | collective-permute-start | bytes 442376 | tf_op jit(solution)/shard_map/ppermute | solution.py:18
  104.4 6.5 %collective-permute-start.9 = (f32[18,1,2,8,128]{4,1,0,2,3:T(1,128)S(1)}, f32[18,1,2,8,128]{4,1,0,2,3:T(1,128)S(1)}, u32[]{:S(2)}, u32[]{:S(2)}) collective-permute-start(f32[18,1,2,8,128]{4,1,0,2,3:T(1,128)S(1)} %get-tuple-element.29), channel_id=1, source_target_pairs={{8,0},{16,8},{24,16},{9,1},{17,9},{25,17},{10,2},{18,10},{26,18},{... | collective-permute-start | bytes 442376 | tf_op jit(solution)/shard_map/ppermute | solution.py:20
  112.7 5.6 collective-permute-start.10
  119.0 6.1 %collective-permute-start.11 = (f32[16,16,1,128]{3,2,1,0:T(1,128)S(1)}, f32[16,16,1,128]{3,2,1,0:T(1,128)S(1)}, u32[]{:S(2)}, u32[]{:S(2)}) collective-permute-start(f32[16,16,1,128]{3,2,1,0:T(1,128)S(1)} %get-tuple-element.74), channel_id=1, source_target_pairs={{1,0},{2,1},{3,2},{4,3},{5,4},{6,5},{7,6},{9,8},{10,9},{11,10},{12... | collective-permute-start | bytes 393224 | tf_op jit(solution)/shard_map/ppermute | solution.py:20
  133.8 7.2 %collective-permute-start.12 = (f32[1,16,2,8,128]{4,1,0,3,2:T(8,128)S(1)}, f32[1,16,2,8,128]{4,1,0,3,2:T(8,128)S(1)}, u32[]{:S(2)}, u32[]{:S(2)}) collective-permute-start(f32[1,16,2,8,128]{4,1,0,3,2:T(8,128)S(1)} %get-tuple-element.40), channel_id=1, source_target_pairs={{0,32},{32,64},{64,96},{96,128},{128,160},{160,192},{192,224},{1,3... | collective-permute-start | bytes 393224 | tf_op jit(solution)/shard_map/ppermute | solution.py:18
  138.4 6.7 %collective-permute-start.13 = (f32[1,16,2,8,128]{4,1,0,3,2:T(8,128)S(1)}, f32[1,16,2,8,128]{4,1,0,3,2:T(8,128)S(1)}, u32[]{:S(2)}, u32[]{:S(2)}) collective-permute-start(f32[1,16,2,8,128]{4,1,0,3,2:T(8,128)S(1)} %get-tuple-element.41), channel_id=1, source_target_pairs={{32,0},{64,32},{96,64},{128,96},{160,128},{192,160},{224,192},{33,... | collective-permute-start | bytes 393224 | tf_op jit(solution)/shard_map/ppermute | solution.py:20
  145.3 7.1 %collective-permute-start.14 = (f32[18,1,2,8,128]{4,1,0,3,2:T(1,128)S(1)}, f32[18,1,2,8,128]{4,1,0,3,2:T(1,128)S(1)}, u32[]{:S(2)}, u32[]{:S(2)}) collective-permute-start(f32[18,1,2,8,128]{4,1,0,3,2:T(1,128)S(1)} %get-tuple-element.24), channel_id=1, source_target_pairs={{0,8},{8,16},{16,24},{1,9},{9,17},{17,25},{2,10},{10,18},{18,26},{... | collective-permute-start | bytes 442376 | tf_op jit(solution)/shard_map/ppermute | solution.py:18
  149.5 6.5 %collective-permute-start.15 = (f32[18,1,2,8,128]{4,1,0,3,2:T(1,128)S(1)}, f32[18,1,2,8,128]{4,1,0,3,2:T(1,128)S(1)}, u32[]{:S(2)}, u32[]{:S(2)}) collective-permute-start(f32[18,1,2,8,128]{4,1,0,3,2:T(1,128)S(1)} %get-tuple-element.25), channel_id=1, source_target_pairs={{8,0},{16,8},{24,16},{9,1},{17,9},{25,17},{10,2},{18,10},{26,18},{... | collective-permute-start | bytes 442376 | tf_op jit(solution)/shard_map/ppermute | solution.py:20
  157.7 7.6 %collective-permute-start.16 = (f32[16,16,1,128]{3,1,0,2:T(8,128)S(1)}, f32[16,16,1,128]{3,1,0,2:T(8,128)S(1)}, u32[]{:S(2)}, u32[]{:S(2)}) collective-permute-start(f32[16,16,1,128]{3,1,0,2:T(8,128)S(1)} %dynamic-slice_bitcast_fusion.1), channel_id=1, source_target_pairs={{0,1},{1,2},{2,3},{3,4},{4,5},{5,6},{6,7},{8,9},{9,10},{10,11},{11... | collective-permute-start | bytes 393224 | tf_op jit(solution)/shard_map/ppermute | solution.py:18
  165.5 6.4 %collective-permute-start.17 = (f32[16,16,1,128]{3,1,0,2:T(8,128)S(1)}, f32[16,16,1,128]{3,1,0,2:T(8,128)S(1)}, u32[]{:S(2)}, u32[]{:S(2)}) collective-permute-start(f32[16,16,1,128]{3,1,0,2:T(8,128)S(1)} %get-tuple-element.70), channel_id=1, source_target_pairs={{1,0},{2,1},{3,2},{4,3},{5,4},{6,5},{7,6},{9,8},{10,9},{11,10},{12... | collective-permute-start | bytes 393224 | tf_op jit(solution)/shard_map/ppermute | solution.py:20
  192.4 6.6 %collective-permute-start.18 = (f32[1,16,2,8,128]{4,1,0,3,2:T(8,128)S(1)}, f32[1,16,2,8,128]{4,1,0,3,2:T(8,128)S(1)}, u32[]{:S(2)}, u32[]{:S(2)}) collective-permute-start(f32[1,16,2,8,128]{4,1,0,3,2:T(8,128)S(1)} %get-tuple-element.32), channel_id=1, source_target_pairs={{0,32},{32,64},{64,96},{96,128},{128,160},{160,192},{192,224},{1,3... | collective-permute-start | bytes 393224 | tf_op jit(solution)/shard_map/ppermute | solution.py:18
  196.1 6.4 %collective-permute-start.19 = (f32[1,16,2,8,128]{4,1,0,3,2:T(8,128)S(1)}, f32[1,16,2,8,128]{4,1,0,3,2:T(8,128)S(1)}, u32[]{:S(2)}, u32[]{:S(2)}) collective-permute-start(f32[1,16,2,8,128]{4,1,0,3,2:T(8,128)S(1)} %get-tuple-element.33), channel_id=1, source_target_pairs={{32,0},{64,32},{96,64},{128,96},{160,128},{192,160},{224,192},{33,... | collective-permute-start | bytes 393224 | tf_op jit(solution)/shard_map/ppermute | solution.py:20
  202.7 6.9 %collective-permute-start.20 = (f32[18,1,2,8,128]{4,1,0,3,2:T(1,128)S(1)}, f32[18,1,2,8,128]{4,1,0,3,2:T(1,128)S(1)}, u32[]{:S(2)}, u32[]{:S(2)}) collective-permute-start(f32[18,1,2,8,128]{4,1,0,3,2:T(1,128)S(1)} %get-tuple-element.22), channel_id=1, source_target_pairs={{0,8},{8,16},{16,24},{1,9},{9,17},{17,25},{2,10},{10,18},{18,26},{... | collective-permute-start | bytes 442376 | tf_op jit(solution)/shard_map/ppermute | solution.py:18
  206.9 6.5 %collective-permute-start.21 = (f32[18,1,2,8,128]{4,1,0,3,2:T(1,128)S(1)}, f32[18,1,2,8,128]{4,1,0,3,2:T(1,128)S(1)}, u32[]{:S(2)}, u32[]{:S(2)}) collective-permute-start(f32[18,1,2,8,128]{4,1,0,3,2:T(1,128)S(1)} %get-tuple-element.23), channel_id=1, source_target_pairs={{8,0},{16,8},{24,16},{9,1},{17,9},{25,17},{10,2},{18,10},{26,18},{... | collective-permute-start | bytes 442376 | tf_op jit(solution)/shard_map/ppermute | solution.py:20
  215.2 9.2 %collective-permute-start.22 = (f32[16,16,1,128]{3,1,0,2:T(8,128)S(1)}, f32[16,16,1,128]{3,1,0,2:T(8,128)S(1)}, u32[]{:S(2)}, u32[]{:S(2)}) collective-permute-start(f32[16,16,1,128]{3,1,0,2:T(8,128)S(1)} %dynamic-slice_bitcast_fusion), channel_id=1, source_target_pairs={{0,1},{1,2},{2,3},{3,4},{4,5},{5,6},{6,7},{8,9},{9,10},{10,11},{11... | collective-permute-start | bytes 393224 | tf_op jit(solution)/shard_map/ppermute | solution.py:18
  224.5 6.4 %collective-permute-start.23 = (f32[16,16,1,128]{3,1,0,2:T(8,128)S(1)}, f32[16,16,1,128]{3,1,0,2:T(8,128)S(1)}, u32[]{:S(2)}, u32[]{:S(2)}) collective-permute-start(f32[16,16,1,128]{3,1,0,2:T(8,128)S(1)} %get-tuple-element.68), channel_id=1, source_target_pairs={{1,0},{2,1},{3,2},{4,3},{5,4},{6,5},{7,6},{9,8},{10,9},{11,10},{12... | collective-permute-start | bytes 393224 | tf_op jit(solution)/shard_map/ppermute | solution.py:20
  (42 other events, 101.5 us)
Sparse Core Ops, SparseCore 0:
  336.8 251.9 all-reduce.46
where the time goes:
time: 610 us; the launch traced here: 601 us
  waiting for transfers between devices  300 us (49%)
  blocking collectives  84.3 us (14%)
  starting transfers between devices  71.9 us (12%)
  other arithmetic  53.6 us (9%)
  matrix products  43.4 us (7%)
  local copies, waits for them, and re-layouts  31.1 us (5%)
  between operations  17 us (3%)
    psum x1, waiting for transfers between devices, on_device(): stacked = lax.psum(stacked, ('gx', 'gy', 'gz'))  246 us
    psum x1, blocking collectives, on_device(): stacked = lax.psum(stacked, ('gx', 'gy', 'gz'))  84.3 us
    ppermute x12, starting transfers between devices, with_halo(): lax.ppermute(tail, axis, [(i, (i + 1) % count) for i in range(ends)])  53.2 us
    ppermute x12, waiting for transfers between devices, with_halo(): lax.ppermute(head, axis, [((i + 1) % count, i) for i in range(ends)])  46.7 us
    dot_general x31, matrix products, matmul_rows(): product = jnp.dot(flattened, weight, preferred_element_type=jnp.float32)  31.6 us
    ppermute x12, starting transfers between devices, with_halo(): lax.ppermute(head, axis, [((i + 1) % count, i) for i in range(ends)])  18.6 us
    unnamed x82, local copies, waits for them, and re-layouts  12.7 us
  transfers between devices with their start and end apart: 25, of which 21 were waited for; matrix products, arithmetic and copies ran while one was open for 3% of the time, Pallas kernels for 0%

commit v1 on v0

--- a/solution.py
+++ b/solution.py
@@ -251,7 +251,7 @@
     stacked = tuple(
         (jnp.stack([per_layer[0][pos_no], per_layer[1][pos_no]]) for pos_no in range(4))
     )
-    stacked = lax.psum(stacked, ("gx", "gy", "gz"))
+    stacked = lax.psum(lax.psum(stacked, ("gy", "gz")), "gx")
     layers_all = 3 * slot_count * size_z // 4
     nodes_all = (
         nodes_edge**3 * elems_x * lax.axis_size("gx") * elems_y * lax.axis_size("gy") * layers_all

time: 610 us -> 480 us (0.79)
  the two profiles are of different devices: /device:TPU:1 before, /device:TPU:16 now
where the time goes in v1:
time: 480 us; the launch traced here: 471 us
  waiting for transfers between devices  185 us (39%)
  blocking collectives  93.8 us (20%)
  other arithmetic  56.9 us (12%)
  starting transfers between devices  51.9 us (11%)
  matrix products  36.2 us (8%)
  local copies, waits for them, and re-layouts  29.5 us (6%)
  between operations  17 us (4%)
    psum x2, waiting for transfers between devices, on_device(): stacked = lax.psum(lax.psum(stacked, ('gy', 'gz')), 'gx')  106 us
    psum x2, blocking collectives, on_device(): stacked = lax.psum(lax.psum(stacked, ('gy', 'gz')), 'gx')  93.8 us
    ppermute x12, waiting for transfers between devices, with_halo(): lax.ppermute(head, axis, [((i + 1) % count, i) for i in range(ends)])  45.9 us
    ppermute x12, waiting for transfers between devices, with_halo(): lax.ppermute(tail, axis, [(i, (i + 1) % count) for i in range(ends)])  33.6 us
    ppermute x12, starting transfers between devices, with_halo(): lax.ppermute(tail, axis, [(i, (i + 1) % count) for i in range(ends)])  33.2 us
    dot_general x31, matrix products, matmul_rows(): product = jnp.dot(flattened, weight, preferred_element_type=jnp.float32)  27.2 us
    ppermute x12, starting transfers between devices, with_halo(): lax.ppermute(head, axis, [((i + 1) % count, i) for i in range(ends)])  18.6 us
    unnamed x68, local copies, waits for them, and re-layouts  11.2 us
  transfers between devices with their start and end apart: 26, of which 20 were waited for; matrix products, arithmetic and copies ran while one was open for 5% of the time, Pallas kernels for 0%

profile of v1, /device:TPU:16, one launch (start us, length us, event | category | flops | bytes accessed | tf_op | source)
XLA Modules:
  0.0 470.7 jit_solution(7676525129523347078)
XLA Ops:
  28.5 3.8 collective-permute-start
  36.0 3.6 collective-permute-done.1
  44.2 3.6 collective-permute-done.3
  52.5 3.4 collective-permute-start.4
  56.2 6.7 %collective-permute-done.4 = f32[16,16,1,128]{3,1,0,2:T(8,128)S(1)} collective-permute-done((f32[16,16,1,128]{3,1,0,2:T(8,128)S(1)}, f32[16,16,1,128]{3,1,0,2:T(8,128)S(1)}, u32[]{:S(2)}, u32[]{:S(2)}) %collective-permute-start.4) | collective-permute-done | bytes 131104 | tf_op jit(solution)/shard_map/ppermute | solution.py:18
  65.3 4.6 collective-permute-done.5
  87.3 3.8 collective-permute-start.6
  94.6 5.5 %collective-permute-done.7 = f32[1,16,2,8,128]{4,1,0,2,3:T(8,128)S(1)} collective-permute-done((f32[1,16,2,8,128]{4,1,0,2,3:T(8,128)S(1)}, f32[1,16,2,8,128]{4,1,0,2,3:T(8,128)S(1)}, u32[]{:S(2)}, u32[]{:S(2)}) %collective-permute-start.7) | collective-permute-done | bytes 131104 | tf_op jit(solution)/shard_map/ppermute | solution.py:20
  103.7 3.7 collective-permute-done.9
  111.3 8.5 %collective-permute-done.10 = f32[16,16,1,128]{3,1,0,2:T(8,128)S(1)} collective-permute-done((f32[16,16,1,128]{3,1,0,2:T(8,128)S(1)}, f32[16,16,1,128]{3,1,0,2:T(8,128)S(1)}, u32[]{:S(2)}, u32[]{:S(2)}) %collective-permute-start.10) | collective-permute-done | bytes 131104 | tf_op jit(solution)/shard_map/ppermute | solution.py:18
  123.8 3.6 collective-permute-done.11
  136.0 4.9 %collective-permute-start.12 = (f32[1,16,2,8,128]{4,1,0,3,2:T(8,128)S(1)}, f32[1,16,2,8,128]{4,1,0,3,2:T(8,128)S(1)}, u32[]{:S(2)}, u32[]{:S(2)}) collective-permute-start(f32[1,16,2,8,128]{4,1,0,3,2:T(8,128)S(1)} %get-tuple-element.43), channel_id=1, source_target_pairs={{0,32},{32,64},{64,96},{96,128},{128,160},{160,192},{192,224},{1,3... | collective-permute-start | bytes 393224 | tf_op jit(solution)/shard_map/ppermute | solution.py:18
  144.3 4.4 collective-permute-done.13
  161.1 7.4 %collective-permute-done.16 = f32[16,16,1,128]{3,1,0,2:T(8,128)S(1)} collective-permute-done((f32[16,16,1,128]{3,1,0,2:T(8,128)S(1)}, f32[16,16,1,128]{3,1,0,2:T(8,128)S(1)}, u32[]{:S(2)}, u32[]{:S(2)}) %collective-permute-start.16) | collective-permute-done | bytes 131104 | tf_op jit(solution)/shard_map/ppermute | solution.py:18
  172.2 3.2 collective-permute-done.17
  193.2 3.9 collective-permute-start.18
  200.6 4.7 collective-permute-done.19
  217.3 7.5 %collective-permute-done.22 = f32[16,16,1,128]{3,1,0,2:T(8,128)S(1)} collective-permute-done((f32[16,16,1,128]{3,1,0,2:T(8,128)S(1)}, f32[16,16,1,128]{3,1,0,2:T(8,128)S(1)}, u32[]{:S(2)}, u32[]{:S(2)}) %collective-permute-start.22) | collective-permute-done | bytes 131104 | tf_op jit(solution)/shard_map/ppermute | solution.py:18
  228.6 3.2 collective-permute-done.23
  249.3 5.8 %subtract_add_fusion = f32[2,8,2,8,2,8,128]{6,5,4,3,2,1,0:T(8,128)S(1)} fusion(f32[2,8,2,8,2,7,128]{6,5,4,3,2,1,0:T(8,128)} %fusion.44, f32[2,8,2,7,2,8,128]{6,5,4,3,2,1,0:T(8,128)} %fusion.129, f32[2,7,2,8,2,8,128]{6,5,4,3,2,1,0:T(8,128)} %fusion.131), kind=kLoop, calls=%fused_computation.58 | loop fusion | flops 2621440 | bytes 7602176 | tf_op jit(solution)/shard_map/add | solution.py:88
  255.1 105.9 %all-reduce.49.cloned.1.call-done = (f32[2,2,128,128]{3,2,1,0:T(8,128)}, f32[2,256,128]{2,1,0:T(8,128)}, f32[2,128,128]{2,1,0:T(8,128)}) async-done(((f32[2,2,128,128]{3,2,1,0:T(8,128)}, f32[2,256,128]{2,1,0:T(8,128)}, f32[2,128,128]{2,1,0:T(8,128)}), (f32[2,2,128,128]{3,2,1,0:T(8,128)}, f32[2,256,128]{2,1,0:T(8,128)}, f32[2,128,128]{2,1,0:T(8,128)})) %all-reduce.49.cloned.1.call-update) | async-done | bytes 655376 | tf_op jit(solution)/shard_map/psum | solution.py:254
  361.1 76.3 %psum.62 = f32[2,2,128]{2,1,0:T(2,128)S(1)} all-reduce(f32[2,2,128]{2,1,0:T(2,128)S(1)} %pad_maximum_fusion.51), channel_id=1, replica_groups=mesh['gx'=8,'gy'=4,'gz'=8] {'gy','gz'}, use_global_device_ids=true, to_apply=%region_14.15 | all-reduce | flops 512 | bytes 4096 | tf_op jit(solution)/shard_map/psum | solution.py:254
  437.4 17.4 %psum.63 = f32[2,2,128]{2,1,0:T(2,128)S(1)} all-reduce(f32[2,2,128]{2,1,0:T(2,128)S(1)} %psum.62), channel_id=1, replica_groups=mesh['gx'=8,'gy'=4,'gz'=8] {'gx'}, use_global_device_ids=true, to_apply=%region_15.16 | all-reduce | flops 512 | bytes 4096 | tf_op jit(solution)/shard_map/psum | solution.py:254
  455.4 3.0 fusion.43
  (330 shorter events, 155.1 us)
Async XLA Ops:
  7.2 353.9 %all-reduce.49.cloned.1.call-start = ((), (), s32[]{:S(2)}) async-start(), calls=%async_computation | async-start | bytes 1310720 | tf_op jit(solution)/shard_map/psum | solution.py:254
  28.5 7.6 %collective-permute-start = (f32[1,16,2,8,128]{4,1,0,3,2:T(8,128)}, f32[1,16,2,8,128]{4,1,0,3,2:T(8,128)S(1)}, u32[]{:S(2)}, u32[]{:S(2)}) collective-permute-start(f32[1,16,2,8,128]{4,1,0,3,2:T(8,128)} %get-tuple-element.59), channel_id=1, source_target_pairs={{0,32},{32,64},{64,96},{96,128},{128,160},{160,192},{192,224},{1,3... | collective-permute-start | bytes 393224 | tf_op jit(solution)/shard_map/ppermute | solution.py:18
  32.3 7.3 %collective-permute-start.1 = (f32[1,16,2,8,128]{4,1,0,3,2:T(8,128)}, f32[1,16,2,8,128]{4,1,0,3,2:T(8,128)}, u32[]{:S(2)}, u32[]{:S(2)}) collective-permute-start(f32[1,16,2,8,128]{4,1,0,3,2:T(8,128)} %get-tuple-element.60), channel_id=1, source_target_pairs={{32,0},{64,32},{96,64},{128,96},{160,128},{192,160},{224,192},{33,... | collective-permute-start | bytes 393224 | tf_op jit(solution)/shard_map/ppermute | solution.py:20
  42.7 5.1 %collective-permute-start.3 = (f32[18,1,2,8,128]{4,1,0,3,2:T(1,128)}, f32[18,1,2,8,128]{4,1,0,3,2:T(1,128)}, u32[]{:S(2)}, u32[]{:S(2)}) collective-permute-start(f32[18,1,2,8,128]{4,1,0,3,2:T(1,128)} %get-tuple-element.34), channel_id=1, source_target_pairs={{8,0},{16,8},{24,16},{9,1},{17,9},{25,17},{10,2},{18,10},{26,18},{... | collective-permute-start | bytes 442376 | tf_op jit(solution)/shard_map/ppermute | solution.py:20
  52.5 10.5 %collective-permute-start.4 = (f32[16,16,1,128]{3,1,0,2:T(8,128)S(1)}, f32[16,16,1,128]{3,1,0,2:T(8,128)S(1)}, u32[]{:S(2)}, u32[]{:S(2)}) collective-permute-start(f32[16,16,1,128]{3,1,0,2:T(8,128)S(1)} %dynamic-slice_bitcast_fusion.3), channel_id=1, source_target_pairs={{0,1},{1,2},{2,3},{3,4},{4,5},{5,6},{6,7},{8,9},{9,10},{10,11},{11... | collective-permute-start | bytes 393224 | tf_op jit(solution)/shard_map/ppermute | solution.py:18
  63.0 6.9 %collective-permute-start.5 = (f32[16,16,1,128]{3,1,0,2:T(8,128)S(1)}, f32[16,16,1,128]{3,1,0,2:T(8,128)S(1)}, u32[]{:S(2)}, u32[]{:S(2)}) collective-permute-start(f32[16,16,1,128]{3,1,0,2:T(8,128)S(1)} %get-tuple-element.79), channel_id=1, source_target_pairs={{1,0},{2,1},{3,2},{4,3},{5,4},{6,5},{7,6},{9,8},{10,9},{11,10},{12... | collective-permute-start | bytes 393224 | tf_op jit(solution)/shard_map/ppermute | solution.py:20
  87.3 7.3 %collective-permute-start.6 = (f32[1,16,2,8,128]{4,1,0,2,3:T(8,128)S(1)}, f32[1,16,2,8,128]{4,1,0,2,3:T(8,128)S(1)}, u32[]{:S(2)}, u32[]{:S(2)}) collective-permute-start(f32[1,16,2,8,128]{4,1,0,2,3:T(8,128)S(1)} %get-tuple-element.51), channel_id=1, source_target_pairs={{0,32},{32,64},{64,96},{96,128},{128,160},{160,192},{192,224},{1,3... | collective-permute-start | bytes 393224 | tf_op jit(solution)/shard_map/ppermute | solution.py:18
  91.1 9.0 %collective-permute-start.7 = (f32[1,16,2,8,128]{4,1,0,2,3:T(8,128)S(1)}, f32[1,16,2,8,128]{4,1,0,2,3:T(8,128)S(1)}, u32[]{:S(2)}, u32[]{:S(2)}) collective-permute-start(f32[1,16,2,8,128]{4,1,0,2,3:T(8,128)S(1)} %get-tuple-element.52), channel_id=1, source_target_pairs={{32,0},{64,32},{96,64},{128,96},{160,128},{192,160},{224,192},{33,... | collective-permute-start | bytes 393224 | tf_op jit(solution)/shard_map/ppermute | solution.py:20
  102.4 5.1 %collective-permute-start.9 = (f32[18,1,2,8,128]{4,1,0,2,3:T(1,128)S(1)}, f32[18,1,2,8,128]{4,1,0,2,3:T(1,128)S(1)}, u32[]{:S(2)}, u32[]{:S(2)}) collective-permute-start(f32[18,1,2,8,128]{4,1,0,2,3:T(1,128)S(1)} %get-tuple-element.32), channel_id=1, source_target_pairs={{8,0},{16,8},{24,16},{9,1},{17,9},{25,17},{10,2},{18,10},{26,18},{... | collective-permute-start | bytes 442376 | tf_op jit(solution)/shard_map/ppermute | solution.py:20
  109.4 10.5 %collective-permute-start.10 = (f32[16,16,1,128]{3,1,0,2:T(8,128)S(1)}, f32[16,16,1,128]{3,1,0,2:T(8,128)S(1)}, u32[]{:S(2)}, u32[]{:S(2)}) collective-permute-start(f32[16,16,1,128]{3,1,0,2:T(8,128)S(1)} %dynamic-slice_bitcast_fusion.2), channel_id=1, source_target_pairs={{0,1},{1,2},{2,3},{3,4},{4,5},{5,6},{6,7},{8,9},{9,10},{10,11},{11... | collective-permute-start | bytes 393224 | tf_op jit(solution)/shard_map/ppermute | solution.py:18
  120.5 6.9 %collective-permute-start.11 = (f32[16,16,1,128]{3,2,1,0:T(1,128)S(1)}, f32[16,16,1,128]{3,2,1,0:T(1,128)S(1)}, u32[]{:S(2)}, u32[]{:S(2)}) collective-permute-start(f32[16,16,1,128]{3,2,1,0:T(1,128)S(1)} %get-tuple-element.77), channel_id=1, source_target_pairs={{1,0},{2,1},{3,2},{4,3},{5,4},{6,5},{7,6},{9,8},{10,9},{11,10},{12... | collective-permute-start | bytes 393224 | tf_op jit(solution)/shard_map/ppermute | solution.py:20
  136.0 8.3 %collective-permute-start.12 = (f32[1,16,2,8,128]{4,1,0,3,2:T(8,128)S(1)}, f32[1,16,2,8,128]{4,1,0,3,2:T(8,128)S(1)}, u32[]{:S(2)}, u32[]{:S(2)}) collective-permute-start(f32[1,16,2,8,128]{4,1,0,3,2:T(8,128)S(1)} %get-tuple-element.43), channel_id=1, source_target_pairs={{0,32},{32,64},{64,96},{96,128},{128,160},{160,192},{192,224},{1,3... | collective-permute-start | bytes 393224 | tf_op jit(solution)/shard_map/ppermute | solution.py:18
  140.9 7.8 %collective-permute-start.13 = (f32[1,16,2,8,128]{4,1,0,3,2:T(8,128)S(1)}, f32[1,16,2,8,128]{4,1,0,3,2:T(8,128)S(1)}, u32[]{:S(2)}, u32[]{:S(2)}) collective-permute-start(f32[1,16,2,8,128]{4,1,0,3,2:T(8,128)S(1)} %get-tuple-element.44), channel_id=1, source_target_pairs={{32,0},{64,32},{96,64},{128,96},{160,128},{192,160},{224,192},{33,... | collective-permute-start | bytes 393224 | tf_op jit(solution)/shard_map/ppermute | solution.py:20
  148.9 4.4 collective-permute-start.14
  151.1 5.1 %collective-permute-start.15 = (f32[18,1,2,8,128]{4,1,0,3,2:T(1,128)S(1)}, f32[18,1,2,8,128]{4,1,0,3,2:T(1,128)S(1)}, u32[]{:S(2)}, u32[]{:S(2)}) collective-permute-start(f32[18,1,2,8,128]{4,1,0,3,2:T(1,128)S(1)} %get-tuple-element.28), channel_id=1, source_target_pairs={{8,0},{16,8},{24,16},{9,1},{17,9},{25,17},{10,2},{18,10},{26,18},{... | collective-permute-start | bytes 442376 | tf_op jit(solution)/shard_map/ppermute | solution.py:20
  158.0 10.5 %collective-permute-start.16 = (f32[16,16,1,128]{3,1,0,2:T(8,128)S(1)}, f32[16,16,1,128]{3,1,0,2:T(8,128)S(1)}, u32[]{:S(2)}, u32[]{:S(2)}) collective-permute-start(f32[16,16,1,128]{3,1,0,2:T(8,128)S(1)} %dynamic-slice_bitcast_fusion.1), channel_id=1, source_target_pairs={{0,1},{1,2},{2,3},{3,4},{4,5},{5,6},{6,7},{8,9},{9,10},{10,11},{11... | collective-permute-start | bytes 393224 | tf_op jit(solution)/shard_map/ppermute | solution.py:18
  168.6 6.9 %collective-permute-start.17 = (f32[16,16,1,128]{3,1,0,2:T(8,128)S(1)}, f32[16,16,1,128]{3,1,0,2:T(8,128)S(1)}, u32[]{:S(2)}, u32[]{:S(2)}) collective-permute-start(f32[16,16,1,128]{3,1,0,2:T(8,128)S(1)} %get-tuple-element.73), channel_id=1, source_target_pairs={{1,0},{2,1},{3,2},{4,3},{5,4},{6,5},{7,6},{9,8},{10,9},{11,10},{12... | collective-permute-start | bytes 393224 | tf_op jit(solution)/shard_map/ppermute | solution.py:20
  193.2 7.4 %collective-permute-start.18 = (f32[1,16,2,8,128]{4,1,0,3,2:T(8,128)S(1)}, f32[1,16,2,8,128]{4,1,0,3,2:T(8,128)S(1)}, u32[]{:S(2)}, u32[]{:S(2)}) collective-permute-start(f32[1,16,2,8,128]{4,1,0,3,2:T(8,128)S(1)} %get-tuple-element.35), channel_id=1, source_target_pairs={{0,32},{32,64},{64,96},{96,128},{128,160},{160,192},{192,224},{1,3... | collective-permute-start | bytes 393224 | tf_op jit(solution)/shard_map/ppermute | solution.py:18
  197.2 8.1 %collective-permute-start.19 = (f32[1,16,2,8,128]{4,1,0,3,2:T(8,128)S(1)}, f32[1,16,2,8,128]{4,1,0,3,2:T(8,128)S(1)}, u32[]{:S(2)}, u32[]{:S(2)}) collective-permute-start(f32[1,16,2,8,128]{4,1,0,3,2:T(8,128)S(1)} %get-tuple-element.36), channel_id=1, source_target_pairs={{32,0},{64,32},{96,64},{128,96},{160,128},{192,160},{224,192},{33,... | collective-permute-start | bytes 393224 | tf_op jit(solution)/shard_map/ppermute | solution.py:20
  205.5 4.0 collective-permute-start.20
  207.5 4.9 %collective-permute-start.21 = (f32[18,1,2,8,128]{4,1,0,3,2:T(1,128)S(1)}, f32[18,1,2,8,128]{4,1,0,3,2:T(1,128)S(1)}, u32[]{:S(2)}, u32[]{:S(2)}) collective-permute-start(f32[18,1,2,8,128]{4,1,0,3,2:T(1,128)S(1)} %get-tuple-element.26), channel_id=1, source_target_pairs={{8,0},{16,8},{24,16},{9,1},{17,9},{25,17},{10,2},{18,10},{26,18},{... | collective-permute-start | bytes 442376 | tf_op jit(solution)/shard_map/ppermute | solution.py:20
  214.3 10.5 %collective-permute-start.22 = (f32[16,16,1,128]{3,1,0,2:T(8,128)S(1)}, f32[16,16,1,128]{3,1,0,2:T(8,128)S(1)}, u32[]{:S(2)}, u32[]{:S(2)}) collective-permute-start(f32[16,16,1,128]{3,1,0,2:T(8,128)S(1)} %dynamic-slice_bitcast_fusion), channel_id=1, source_target_pairs={{0,1},{1,2},{2,3},{3,4},{4,5},{5,6},{6,7},{8,9},{9,10},{10,11},{11... | collective-permute-start | bytes 393224 | tf_op jit(solution)/shard_map/ppermute | solution.py:18
  224.9 6.9 %collective-permute-start.23 = (f32[16,16,1,128]{3,1,0,2:T(8,128)S(1)}, f32[16,16,1,128]{3,1,0,2:T(8,128)S(1)}, u32[]{:S(2)}, u32[]{:S(2)}) collective-permute-start(f32[16,16,1,128]{3,1,0,2:T(8,128)S(1)} %get-tuple-element.71), channel_id=1, source_target_pairs={{1,0},{2,1},{3,2},{4,3},{5,4},{6,5},{7,6},{9,8},{10,9},{11,10},{12... | collective-permute-start | bytes 393224 | tf_op jit(solution)/shard_map/ppermute | solution.py:20
  249.2 209.3 %all-reduce.51.cloned.1.call-start = ((), (), s32[]{:S(2)}) async-start(), calls=%async_computation.1 | async-start | bytes 1310720 | tf_op jit(solution)/shard_map/psum | solution.py:254
  (36 other events, 271.1 us)
Sparse Core Ops, SparseCore 0:
  249.3 111.6 all-reduce.48
  363.6 74.7 all-reduce.50
